TPU v7x, 512 devices: a whole 4x8x8 slice. The times are simulated.
512 devices in a mesh: dp: 16 (over z, core), head: 8 (over y), tok: 4 (over x).
Axes of the slice: x: 4, y: 8, z: 8, core: 2. Of those that a mesh axis runs over, the one named last changes fastest.
Arguments:
- mamba_input: bfloat16 [32, 64, 8192], P('dp', 'tok', 'head'), may hold values from -6 to 6
- gate_input: bfloat16 [32, 64, 8192], P('dp', 'tok', 'head'), may hold values from -6 to 6
- in_b: bfloat16 [32, 64, 1024], P('dp', 'tok', 'head'), may hold values from -0.75 to 0.75
- in_c: bfloat16 [32, 64, 1024], P('dp', 'tok', 'head'), may hold values from -0.75 to 0.75
- step_size: bfloat16 [32, 64, 128], P('dp', 'tok', 'head'), may hold values from 0.019897461 to 1
- decay_rate: float32 [128], P('head'), may hold values from 0.01 to 1
- skip_weight: float32 [128], P('head'), may hold values from 0.5 to 1.5
- norm_gain: float32 [8192], P('head'), may hold values from 0.1 to 1.9
- ssm_state: bfloat16 [32, 128, 64, 128], P('dp', 'head', None, 'tok'), may hold values from -6 to 6
- out_weight: bfloat16 [8192, 4096], P(('head', 'tok')), may hold values from -0.0625 to 0.0625
- queries: bfloat16 [32, 64, 4096], P('dp', 'tok', 'head'), may hold values from -6 to 6
- draft_token_keys: bfloat16 [32, 64, 1024], P('dp', 'tok', 'head'), may hold values from -6 to 6
- draft_values: bfloat16 [32, 64, 1024], P('dp', 'tok', 'head'), may hold values from -6 to 6
- cached_key_rows: bfloat16 [32, 4096, 1024], P('dp', 'tok', 'head'), may hold values from -4 to 4
- cache_values: bfloat16 [32, 4096, 1024], P('dp', 'tok', 'head'), may hold values from -6 to 6
- cache_len: int32 [32], P('dp'), may hold values from 2 to 4096
- accepted: int32 [32], P('dp'), may hold values from 0 to 64
Outputs:
- mamba_out: bfloat16 [64, 32, 4096], P(('head', 'tok'), 'dp')
- attn_context: bfloat16 [32, 64, 4096], P('dp', 'tok', 'head')
- committed_state: bfloat16 [32, 128, 64, 128], P('dp', 'head', None, 'tok')
Inputs may be any that keep to these rules, and one draw needn't show every extreme that they name: Each sequence's cached positions 0 to cache_len - 1 are valid.
All inputs are finite; a program needn't handle non-finite values.
Results may differ from a plain program's by a relative error of at most 0.018.
Values may be sent and summed in bfloat16 or wider, within the bound.
No kernel may reach another device: no remote copies, remote signals or barrier semaphores. Data moves between devices by JAX's collectives and lax.ppermute only.
A program may use at most 64 MiB of HBM per device.

v0:
```python
import jax
import jax.numpy as jnp
from jax import lax
from jax.sharding import PartitionSpec as P

EPSILON = 1e-05
MASKED = -1e30


def in_one_piece(arrays, axis, split_dim, concat_dim, along):
    widths = [a.shape[along] for a in arrays]
    both = jnp.concatenate(arrays, axis=along)
    filled = lax.all_to_all(both, axis, split_axis=split_dim, concat_axis=concat_dim, tiled=True)
    return tuple(jnp.split(filled, [sum(widths[:k]) for k in range(1, len(widths))], axis=along))


def sent_together(arrays, axis, dim, along):
    widths = [a.shape[along] for a in arrays]
    both = jnp.concatenate(arrays, axis=along)
    filled = lax.all_gather(both, axis, axis=dim, tiled=True)
    return tuple(jnp.split(filled, [sum(widths[:k]) for k in range(1, len(widths))], axis=along))


def in_blocks(array, dim, count):
    before, after = (array.shape[:dim], array.shape[dim + 1 :])
    return jnp.moveaxis(array.reshape(*before, count, -1, *after), dim, 0)


def summed_on_arrival(array, axis, dim):
    parts = in_blocks(array, dim, lax.axis_size(axis))
    arrived = lax.all_to_all(parts, axis, split_axis=0, concat_axis=0, tiled=True)
    return arrived.astype(jnp.float32).sum(axis=0)


def from_everyone(array, axis):
    copies = jnp.broadcast_to(array, (lax.axis_size(axis), *array.shape))
    return lax.all_to_all(copies, axis, split_axis=0, concat_axis=0, tiled=True)


def laid_out(parts, dim):
    parts = jnp.moveaxis(parts, 0, dim)
    shape = parts.shape
    return parts.reshape(*shape[:dim], shape[dim] * shape[dim + 1], *shape[dim + 2 :])


def gather_directly(array, axis, dim):
    parts = from_everyone(array, axis)
    return laid_out(parts, dim)


def within_block(running, step_sizes, feature_values, inflow, readout):
    count = running.shape[1]
    position = jnp.arange(count)
    causal = (position[:, None] >= position[None, :])[None, :, :, None]
    log_gaps = jnp.where(causal, running[:, :, None, :] - running[:, None, :, :], 0.0)
    decays = jnp.where(causal, jnp.exp(log_gaps), 0.0)
    affinity = jnp.einsum("bsn,brn->bsr", readout, inflow)
    mixing = affinity[..., None] * decays * step_sizes[:, None, :, :]
    return jnp.einsum("bsrh,brhp->bshp", mixing, feature_values)


def select_state(limit, log_decay, running, step_sizes, feature_values, inflow, start_state):
    count = running.shape[1]
    alive = (jnp.arange(count)[None, :] < limit[:, None])[..., None]
    end_log = jnp.sum(jnp.where(alive, log_decay, 0.0), axis=1)
    weights = jnp.where(
        alive, jnp.exp(jnp.where(alive, end_log[:, None, :] - running, 0.0)) * step_sizes, 0.0
    )
    return jnp.exp(end_log)[..., None, None] * start_state + jnp.einsum(
        "brh,brhp,brn->bhpn", weights, feature_values, inflow
    )


def body(
    mamba_input,
    gate_input,
    in_b,
    in_c,
    step_size,
    decay_rate,
    skip_weight,
    norm_gain,
    ssm_state,
    out_weight,
    queries,
    draft_token_keys,
    draft_values,
    cached_key_rows,
    cache_values,
    cache_len,
    accepted,
):
    sequences, block_len, feature_width = mamba_input.shape
    head_count = decay_rate.shape[0]
    head_size = feature_width // head_count
    tok_count = lax.axis_size("tok")
    tok_index = lax.axis_index("tok")
    first_draft = tok_index * block_len
    feature_values = mamba_input.astype(jnp.float32).reshape(
        sequences, block_len, head_count, head_size
    )
    inflow_cols, readout_cols = in_one_piece((in_b, in_c), "tok", 2, 1, 0)
    all_inputs, all_steps = sent_together((mamba_input, step_size), "tok", 1, 2)
    draft_len = all_inputs.shape[1]
    all_features = all_inputs.astype(jnp.float32).reshape(
        sequences, draft_len, head_count, head_size
    )
    step_sizes = all_steps.astype(jnp.float32)
    inflow = inflow_cols.astype(jnp.float32)
    readout = readout_cols.astype(jnp.float32)
    log_decay = -step_sizes * decay_rate[None, None, :]
    running = jnp.cumsum(log_decay, axis=1)
    within = within_block(running, step_sizes, all_features, inflow, readout)
    start_state = ssm_state.astype(jnp.float32)
    carried = jnp.einsum("bsn,bhpn->bshp", readout, start_state) * jnp.exp(running)[..., None]
    partial_sum = (within + carried).reshape(sequences, draft_len, feature_width)
    mixed = summed_on_arrival(partial_sum.astype(jnp.bfloat16), "tok", 1).reshape(
        sequences, block_len, head_count, head_size
    )
    chosen = select_state(
        accepted, log_decay, running, step_sizes, all_features, inflow, start_state
    )
    committed_state = chosen.astype(jnp.bfloat16)
    mixed = mixed + skip_weight[None, None, :, None] * feature_values
    gated = mixed.reshape(sequences, block_len, feature_width) * jax.nn.silu(
        gate_input.astype(jnp.float32)
    )
    mean_sq = jnp.mean(gated * gated, axis=-1, keepdims=True)
    normed = (gated * lax.rsqrt(mean_sq + EPSILON) * norm_gain).astype(jnp.bfloat16)
    regrouped = lax.all_to_all(normed, "tok", split_axis=2, concat_axis=1, tiled=True)
    mamba_out = summed_on_arrival(
        jnp.einsum("sdf,fo->dso", regrouped, out_weight, preferred_element_type=jnp.float32).astype(
            jnp.bfloat16
        ),
        ("head", "tok"),
        0,
    ).astype(jnp.bfloat16)
    all_queries = gather_directly(queries, "tok", 1)
    att_size = draft_token_keys.shape[2]
    per_kv = queries.shape[2] // att_size
    draft_len = all_queries.shape[1]
    cache_block = cached_key_rows.shape[1]
    query_matrix = all_queries.reshape(sequences, draft_len * per_kv, att_size)
    score_scale = att_size ** (-0.5)
    cache_scores = (
        jnp.einsum(
            "cmq,czq->cmz", query_matrix, cached_key_rows, preferred_element_type=jnp.float32
        )
        * score_scale
    )
    draft_scores = (
        jnp.einsum(
            "cmq,czq->cmz", query_matrix, draft_token_keys, preferred_element_type=jnp.float32
        )
        * score_scale
    )
    cache_pos = tok_index * cache_block + jnp.arange(cache_block)
    cache_valid = cache_pos[None, None, :] < cache_len[:, None, None]
    query_pos = jnp.repeat(jnp.arange(draft_len), per_kv)
    draft_valid = ((first_draft + jnp.arange(block_len))[None, :] <= query_pos[:, None])[None, :, :]
    cache_scores = jnp.where(cache_valid, cache_scores, MASKED)
    draft_scores = jnp.where(draft_valid, draft_scores, MASKED)
    row_peak = jnp.maximum(jnp.max(cache_scores, axis=-1), jnp.max(draft_scores, axis=-1))
    cache_probs = jnp.where(cache_valid, jnp.exp(cache_scores - row_peak[..., None]), 0.0)
    draft_probs = jnp.where(draft_valid, jnp.exp(draft_scores - row_peak[..., None]), 0.0)
    row_total = jnp.sum(cache_probs, axis=-1) + jnp.sum(draft_probs, axis=-1)
    numer = jnp.einsum(
        "ces,csx->cex",
        cache_probs.astype(jnp.bfloat16),
        cache_values,
        preferred_element_type=jnp.float32,
    )
    numer = numer + jnp.einsum(
        "ces,csx->cex",
        draft_probs.astype(jnp.bfloat16),
        draft_values,
        preferred_element_type=jnp.float32,
    )
    peaks, totals, numers = tuple(
        (
            part.astype(jnp.float32)
            for part in in_one_piece(
                (
                    row_peak.reshape(1, sequences, draft_len, per_kv).astype(jnp.bfloat16),
                    row_total.reshape(1, sequences, draft_len, per_kv).astype(jnp.bfloat16),
                    numer.reshape(1, sequences, draft_len, per_kv * att_size).astype(jnp.bfloat16),
                ),
                "tok",
                2,
                0,
                3,
            )
        )
    )
    overall = jnp.max(peaks, axis=0)
    rescale = jnp.exp(peaks - overall[None])
    denominator = jnp.sum(rescale * totals, axis=0)
    numers = numers.reshape(tok_count, sequences, block_len, per_kv, att_size)
    context = jnp.sum(rescale[..., None] * numers, axis=0) / denominator[..., None]
    attn_context = context.reshape(sequences, block_len, per_kv * att_size).astype(jnp.bfloat16)
    return (mamba_out, attn_context, committed_state)


def solution(mesh):
    in_specs = (
        P("dp", "tok", "head"),
        P("dp", "tok", "head"),
        P("dp", "tok", "head"),
        P("dp", "tok", "head"),
        P("dp", "tok", "head"),
        P("head"),
        P("head"),
        P("head"),
        P("dp", "head", None, "tok"),
        P(("head", "tok"), None),
        P("dp", "tok", "head"),
        P("dp", "tok", "head"),
        P("dp", "tok", "head"),
        P("dp", "tok", "head"),
        P("dp", "tok", "head"),
        P("dp"),
        P("dp"),
    )
    out_specs = (
        P(("head", "tok"), "dp", None),
        P("dp", "tok", "head"),
        P("dp", "head", None, "tok"),
    )
    return jax.shard_map(body, mesh=mesh, in_specs=in_specs, out_specs=out_specs, check_vma=False)
```

profile of v0, /device:TPU:450, one launch (start us, length us, event | category | flops | bytes accessed | tf_op | source)
XLA Modules:
  0.0 98.2 jit_solution(13853714180560108559)
XLA Ops:
  0.7 0.9 pad_maximum_fusion.2
  1.7 0.8 reshape.233
  2.4 4.8 %all-to-all-start = ((bf16[4,2,1024]{2,1,0:T(2,128)(2,1)}), bf16[4,2,1024]{2,1,0:T(2,128)(2,1)S(1)}, u32[]{:S(2)}, u32[]{:S(2)}) async-start(bf16[4,2,1024]{2,1,0:T(2,128)(2,1)} %reshape.233), calls=%async_computation | async-start | bytes 32768 | tf_op jit(solution)/shard_map/all_to_all | solution.py:13
  7.4 0.9 pad_maximum_fusion.1
  8.3 12.6 %all_gather.3 = bf16[2,64,1040]{2,1,0:T(8,128)(2,1)S(1)} all-gather(bf16[2,16,1040]{2,1,0:T(8,128)(2,1)S(1)} %pad_maximum_fusion.1), channel_id=1, replica_groups=mesh['dp'=16,'head'=8,'tok'=4] {'tok'}, dimensions={1}, use_global_device_ids=true | all-gather | bytes 332800 | tf_op jit(solution)/shard_map/all_gather | solution.py:20
  20.9 0.7 iota_compare_fusion.1
  21.6 0.7 broadcast_compare_fusion.1
  22.4 0.8 select_reduce_fusion
  24.1 0.7 broadcast_in_dim.109
  24.8 4.5 %all-to-all-start.4 = ((bf16[4,2,16,512]{3,2,1,0:T(8,128)(2,1)}), bf16[4,2,16,512]{3,2,1,0:T(8,128)(2,1)S(1)}, u32[]{:S(2)}, u32[]{:S(2)}) async-start(bf16[4,2,16,512]{3,2,1,0:T(8,128)(2,1)} %broadcast_in_dim.109), calls=%async_computation.4 | async-start | bytes 262144 | tf_op jit(solution)/shard_map/all_to_all | solution.py:37
  30.2 1.3 %fusion.6 = bf16[2,64,16,64]{1,3,2,0:T(8,128)(2,1)S(1)} fusion(f32[2,64,16,64]{1,3,2,0:T(8,128)S(1)} %convolution_bitcast_fusion, bf16[2,64,32,1]{2,1,3,0:T(8,128)(2,1)S(1)} %bitcast.67, bf16[2,16,64,32]{2,3,1,0:T(8,128)(2,1)} %param.25, f32[2,64,16]{1,2,0:T(8,128)S(1)} %copy.84), kind=kOutput, calls=%fused_computation.11 | convolution fusion | flops 8781824 | bytes 933888 | tf_op jit(solution)/shard_map/bsn,bhpn->bshp/dot_general | solution.py:115
  32.3 0.7 copy.87
  33.0 0.7 all-to-all-done.4
  33.8 4.8 %all-to-all-start.1 = ((bf16[4,2,16,1024]{3,2,1,0:T(8,128)(2,1)}), bf16[4,2,16,1024]{3,2,1,0:T(8,128)(2,1)S(1)}, u32[]{:S(2)}, u32[]{:S(2)}) async-start(bf16[4,2,16,1024]{3,2,1,0:T(8,128)(2,1)} %copy.87), calls=%async_computation.1 | async-start | bytes 524288 | tf_op jit(solution)/shard_map/all_to_all | solution.py:31
  38.7 1.6 %fusion.2 = (f32[2,256]{1,0:T(2,128)S(1)}, f32[2,256,1024]{2,1,0:T(8,128)S(1)}) fusion(pred[2,1024]{1,0:T(4,128)(4,1)S(1)} %broadcast_compare_fusion.1, bf16[2,256,128]{2,1,0:T(8,128)(2,1)S(1)} %reshape_reshape.3, bf16[2,1024,128]{2,1,0:T(8,128)(2,1)} %param.30), kind=kOutput, calls=%fused_computation.5 | convolution fusion | flops 135790080 | bytes 2756608 | tf_op jit(solution)/shard_map/cmq,czq->cmz/dot_general | solution.py:146
  41.5 0.7 fusion.8
  42.8 1.1 %all-to-all-done.1 = bf16[4,2,16,1024]{3,2,1,0:T(8,128)(2,1)S(1)} async-done(((bf16[4,2,16,1024]{3,2,1,0:T(8,128)(2,1)}), bf16[4,2,16,1024]{3,2,1,0:T(8,128)(2,1)S(1)}, u32[]{:S(2)}, u32[]{:S(2)}) %all-to-all-start.1) | async-done | bytes 262176 | tf_op jit(solution)/shard_map/all_to_all | solution.py:31
  44.5 1.2 %reshape.235 = bf16[4,2,4096]{2,1,0:T(2,128)(2,1)} reshape(bf16[1024,2,16]{2,1,0:T(2,128)(2,1)S(1)} %bitcast.55) | data formatting | bytes 131072
  45.7 4.7 %all-to-all-start.2 = ((bf16[4,2,4096]{2,1,0:T(2,128)(2,1)}), bf16[4,2,4096]{2,1,0:T(2,128)(2,1)S(1)}, u32[]{:S(2)}, u32[]{:S(2)}) async-start(bf16[4,2,4096]{2,1,0:T(2,128)(2,1)} %reshape.235), calls=%async_computation.2 | async-start | bytes 131072 | tf_op jit(solution)/shard_map/all_to_all | solution.py:130
  50.4 1.1 %pad_maximum_fusion = bf16[1,2,64,520]{3,1,0,2:T(2,128)(2,1)} fusion(bf16[1,2,64,512]{3,1,0,2:T(2,128)(2,1)S(1)} %copy.95, bf16[1,2,64,4]{3,1,0,2:T(2,128)(2,1)S(1)} %copy.94, bf16[1,2,64,4]{3,1,0,2:T(2,128)(2,1)S(1)} %copy.93), kind=kLoop, calls=%fused_computation.41 | loop fusion | flops 399360 | bytes 266240 | tf_op jit(solution)/shard_map/concatenate | solution.py:12
  51.5 3.1 %all-to-all-done.2 = bf16[4,2,4096]{2,1,0:T(2,128)(2,1)S(1)} async-done(((bf16[4,2,4096]{2,1,0:T(2,128)(2,1)}), bf16[4,2,4096]{2,1,0:T(2,128)(2,1)S(1)}, u32[]{:S(2)}, u32[]{:S(2)}) %all-to-all-start.2) | async-done | bytes 65568 | tf_op jit(solution)/shard_map/all_to_all | solution.py:130
  54.6 4.8 %all-to-all-start.5 = ((bf16[1,2,64,520]{3,1,0,2:T(2,128)(2,1)}), bf16[1,2,64,520]{3,1,0,2:T(2,128)(2,1)S(1)}, u32[]{:S(2)}, u32[]{:S(2)}) async-start(bf16[1,2,64,520]{3,1,0,2:T(2,128)(2,1)} %pad_maximum_fusion), calls=%async_computation.5 | async-start | bytes 327680 | tf_op jit(solution)/shard_map/all_to_all | solution.py:13
  60.5 1.5 %reshape.230 = bf16[32,2,2,4096]{3,1,0,2:T(2,128)(2,1)} reshape(bf16[64,2,4096]{2,0,1:T(8,128)(2,1)S(1)} %fusion) | data formatting | bytes 2097152 | tf_op jit(solution)/shard_map/reshape | solution.py:26
  62.0 3.4 %copy.90 = bf16[32,2,2,4096]{3,1,2,0:T(2,128)(2,1)} copy(bf16[32,2,2,4096]{3,1,0,2:T(2,128)(2,1)} %reshape.230) | data formatting | bytes 2097152 | tf_op jit(solution)/shard_map/reshape | solution.py:26
  65.4 10.2 %all-to-all-start.3 = ((bf16[32,2,2,4096]{3,1,2,0:T(2,128)(2,1)}), bf16[32,2,2,4096]{3,1,2,0:T(2,128)(2,1)S(1)}, u32[]{:S(2)}, u32[]{:S(2)}) async-start(bf16[32,2,2,4096]{3,1,2,0:T(2,128)(2,1)} %copy.90), calls=%async_computation.3 | async-start | bytes 2097152 | tf_op jit(solution)/shard_map/all_to_all | solution.py:31
  75.8 2.2 %fusion.7 = bf16[2,16,64,32]{2,3,1,0:T(8,128)(2,1)} fusion(bf16[2,64,16,64]{1,3,2,0:T(8,128)(2,1)} %bitcast.62, bf16[2,16,64,32]{2,3,1,0:T(8,128)(2,1)} %param.25, f32[2,64,16]{1,2,0:T(8,128)S(1)} %copy.97, f32[2,64,32]{1,2,0:T(8,128)S(1)} %copy.96, f32[2,16]{1,0:T(2,128)S(1)} %exp.39), kind=kOutput, calls=%fused_computation.13 | convolution fusion | flops 8716288 | bytes 548992 | tf_op jit(solution)/shard_map/brh,brhp,brn->bhpn/dot_general | solution.py:69
  78.3 0.9 mul.139
  79.2 1.1 %mul.140 = f32[4,2,16,512]{3,1,2,0:T(2,128)S(1)} reshape(f32[4,2,16,4,128]{4,3,1,2,0:T(4,128)} %mul.139) | data formatting | bytes 524288 | tf_op jit(solution)/shard_map/mul | solution.py:199
  80.5 1.2 %multiply_reduce_fusion = f32[2,16,512]{2,0,1:T(2,128)S(1)} fusion(f32[4,2,16,512]{3,1,2,0:T(2,128)S(1)} %mul.140, bf16[4,2,16,520]{3,1,2,0:T(2,128)(2,1)} %bitcast.60), kind=kLoop, calls=%fused_computation.38 | loop fusion | flops 180224 | bytes 458752 | tf_op jit(solution)/shard_map/reduce_sum | solution.py:199
  82.4 14.1 %all-to-all-done.3 = bf16[32,2,2,4096]{3,1,2,0:T(2,128)(2,1)S(1)} async-done(((bf16[32,2,2,4096]{3,1,2,0:T(2,128)(2,1)}), bf16[32,2,2,4096]{3,1,2,0:T(2,128)(2,1)S(1)}, u32[]{:S(2)}, u32[]{:S(2)}) %all-to-all-start.3) | async-done | bytes 1048608 | tf_op jit(solution)/shard_map/all_to_all | solution.py:31
  96.5 1.0 %reduce_sum.77 = bf16[2,2,4096]{2,0,1:T(2,128)(2,1)S(1)} reduce(bf16[32,2,2,4096]{3,1,2,0:T(2,128)(2,1)S(1)} %all-to-all-done.3, bf16[]{:T(256)} %constant.10.clone.1), dimensions={0}, to_apply=%region_3.4 | reduce | flops 507904 | bytes 1081346 | tf_op jit(solution)/shard_map/reduce_sum | solution.py:32
  97.5 0.7 copy.99
  (81 shorter events, 7.6 us)
Async XLA Ops:
  0.6 59.4 %copy-start = (bf16[256,4096]{1,0:T(8,128)(2,1)S(1)}, bf16[256,4096]{1,0:T(8,128)(2,1)}, u32[]{:S(2)}) copy-start(bf16[256,4096]{1,0:T(8,128)(2,1)} %param.26) | copy-start | bytes 6291460
  0.6 23.3 %copy-start.9 = (f32[16]{0:T(128)S(1)}, f32[16]{0:T(128)}, u32[]{:S(2)}) copy-start(f32[16]{0:T(128)} %param.23) | copy-start | bytes 196
  0.7 23.4 %copy-start.5 = (bf16[2,16,512]{2,1,0:T(8,128)(2,1)S(1)}, bf16[2,16,512]{2,1,0:T(8,128)(2,1)}, u32[]{:S(2)}) copy-start(bf16[2,16,512]{2,1,0:T(8,128)(2,1)} %param.27) | copy-start | bytes 98308
  2.4 21.6 %all-to-all-start = ((bf16[4,2,1024]{2,1,0:T(2,128)(2,1)}), bf16[4,2,1024]{2,1,0:T(2,128)(2,1)S(1)}, u32[]{:S(2)}, u32[]{:S(2)}) async-start(bf16[4,2,1024]{2,1,0:T(2,128)(2,1)} %reshape.233), calls=%async_computation | async-start | bytes 32768 | tf_op jit(solution)/shard_map/all_to_all | solution.py:13
  23.8 6.4 %copy-start.2 = (bf16[2,64,1024]{1,2,0:T(8,128)(2,1)}, bf16[2,64,1024]{1,2,0:T(8,128)(2,1)S(1)}, u32[]{:S(2)}) copy-start(bf16[2,64,1024]{1,2,0:T(8,128)(2,1)S(1)} %copy.75) | copy-start | bytes 786436
  24.8 9.0 %all-to-all-start.4 = ((bf16[4,2,16,512]{3,2,1,0:T(8,128)(2,1)}), bf16[4,2,16,512]{3,2,1,0:T(8,128)(2,1)S(1)}, u32[]{:S(2)}, u32[]{:S(2)}) async-start(bf16[4,2,16,512]{3,2,1,0:T(8,128)(2,1)} %broadcast_in_dim.109), calls=%async_computation.4 | async-start | bytes 262144 | tf_op jit(solution)/shard_map/all_to_all | solution.py:37
  32.3 8.1 %copy-start.6 = (bf16[2,16,128]{2,1,0:T(8,128)(2,1)S(1)}, bf16[2,16,128]{2,1,0:T(8,128)(2,1)}, u32[]{:S(2)}) copy-start(bf16[2,16,128]{2,1,0:T(8,128)(2,1)} %param.28) | copy-start | bytes 24580
  33.0 7.6 %copy-start.7 = (bf16[2,16,128]{2,1,0:T(8,128)(2,1)S(1)}, bf16[2,16,128]{2,1,0:T(8,128)(2,1)}, u32[]{:S(2)}) copy-start(bf16[2,16,128]{2,1,0:T(8,128)(2,1)} %param.29) | copy-start | bytes 24580
  33.8 10.1 %all-to-all-start.1 = ((bf16[4,2,16,1024]{3,2,1,0:T(8,128)(2,1)}), bf16[4,2,16,1024]{3,2,1,0:T(8,128)(2,1)S(1)}, u32[]{:S(2)}, u32[]{:S(2)}) async-start(bf16[4,2,16,1024]{3,2,1,0:T(8,128)(2,1)} %copy.87), calls=%async_computation.1 | async-start | bytes 524288 | tf_op jit(solution)/shard_map/all_to_all | solution.py:31
  38.7 2.8 %copy-start.10 = (bf16[2,1024,128]{2,1,0:T(8,128)(2,1)S(1)}, bf16[2,1024,128]{2,1,0:T(8,128)(2,1)}, u32[]{:S(2)}) copy-start(bf16[2,1024,128]{2,1,0:T(8,128)(2,1)} %param.31) | copy-start | bytes 1572868
  41.5 2.4 %copy-start.3 = (bf16[2,16,1024]{2,1,0:T(8,128)(2,1)S(1)}, bf16[2,16,1024]{2,1,0:T(8,128)(2,1)}, u32[]{:S(2)}) copy-start(bf16[2,16,1024]{2,1,0:T(8,128)(2,1)} %param.17) | copy-start | bytes 196612
  41.5 2.4 %copy-start.4 = (bf16[2,16,1024]{2,1,0:T(8,128)(2,1)S(1)}, bf16[2,16,1024]{2,1,0:T(8,128)(2,1)}, u32[]{:S(2)}) copy-start(bf16[2,16,1024]{2,1,0:T(8,128)(2,1)} %param.18) | copy-start | bytes 196612
  41.5 2.5 %copy-start.8 = (f32[1024]{0:T(1024)S(1)}, f32[1024]{0:T(1024)}, u32[]{:S(2)}) copy-start(f32[1024]{0:T(1024)} %param.24) | copy-start | bytes 12292
  45.7 8.9 %all-to-all-start.2 = ((bf16[4,2,4096]{2,1,0:T(2,128)(2,1)}), bf16[4,2,4096]{2,1,0:T(2,128)(2,1)S(1)}, u32[]{:S(2)}, u32[]{:S(2)}) async-start(bf16[4,2,4096]{2,1,0:T(2,128)(2,1)} %reshape.235), calls=%async_computation.2 | async-start | bytes 131072 | tf_op jit(solution)/shard_map/all_to_all | solution.py:130
  54.6 10.8 %all-to-all-start.5 = ((bf16[1,2,64,520]{3,1,0,2:T(2,128)(2,1)}), bf16[1,2,64,520]{3,1,0,2:T(2,128)(2,1)S(1)}, u32[]{:S(2)}, u32[]{:S(2)}) async-start(bf16[1,2,64,520]{3,1,0,2:T(2,128)(2,1)} %pad_maximum_fusion), calls=%async_computation.5 | async-start | bytes 327680 | tf_op jit(solution)/shard_map/all_to_all | solution.py:13
  65.4 12.8 %copy-start.1 = (bf16[1,2,64,520]{3,1,0,2:T(2,128)(2,1)}, bf16[1,2,64,520]{3,1,0,2:T(2,128)(2,1)S(1)}, u32[]{:S(2)}) copy-start(bf16[1,2,64,520]{3,1,0,2:T(2,128)(2,1)S(1)} %all-to-all-done.5) | copy-start | bytes 399364
  65.4 31.1 %all-to-all-start.3 = ((bf16[32,2,2,4096]{3,1,2,0:T(2,128)(2,1)}), bf16[32,2,2,4096]{3,1,2,0:T(2,128)(2,1)S(1)}, u32[]{:S(2)}, u32[]{:S(2)}) async-start(bf16[32,2,2,4096]{3,1,2,0:T(2,128)(2,1)} %copy.90), calls=%async_computation.3 | async-start | bytes 2097152 | tf_op jit(solution)/shard_map/all_to_all | solution.py:31
where the time goes:
time: 99.1 us; the launch traced here: 98.2 us
  starting transfers between devices  33.9 us (34%)
  waiting for transfers between devices  19 us (19%)
  local copies, waits for them, and re-layouts  15.6 us (16%)
  blocking collectives  12.6 us (13%)
  other arithmetic  8.71 us (9%)
  matrix products  7.29 us (7%)
  between operations  1.06 us (1%)
    all_to_all x2, waiting for transfers between devices, summed_on_arrival(): lax.all_to_all(parts, axis, split_axis=0, concat_axis=0, tiled=True)  15.2 us
    all_to_all x2, starting transfers between devices, summed_on_arrival(): lax.all_to_all(parts, axis, split_axis=0, concat_axis=0, tiled=True)  15.1 us
    all_gather x1, blocking collectives, sent_together(): filled = lax.all_gather(both, axis, axis=dim, tiled=True)  12.6 us
    all_to_all x2, starting transfers between devices, in_one_piece(): lax.all_to_all(both, axis, split_axis=split_dim, concat_axis=concat_dim,...  9.59 us
    reshape x2, local copies, waits for them, and re-layouts, in_blocks(): return jnp.moveaxis(array.reshape(*before, count, -1, *after), dim, 0)  4.9 us
    all_to_all x1, starting transfers between devices, body(): lax.all_to_all(normed, 'tok', split_axis=2, concat_axis=1, tiled=True)  4.71 us
    all_to_all x1, starting transfers between devices, from_everyone(): return lax.all_to_all(copies, axis, split_axis=0, concat_axis=0, tiled=True)  4.5 us
    unnamed x28, local copies, waits for them, and re-layouts  3.78 us
  transfers between devices with their start and end apart: 6, of which 4 were waited for; matrix products, arithmetic and copies ran while one was open for 26% of the time, Pallas kernels for 0%

commit v1 on v0

--- a/solution.py
+++ b/solution.py
@@ -127,7 +127,10 @@
     )
     mean_sq = jnp.mean(gated * gated, axis=-1, keepdims=True)
     normed = (gated * lax.rsqrt(mean_sq + EPSILON) * norm_gain).astype(jnp.bfloat16)
-    regrouped = lax.all_to_all(normed, "tok", split_axis=2, concat_axis=1, tiled=True)
+    regrouped = jnp.concatenate(
+        lax.all_to_all(jnp.stack(jnp.split(normed, lax.axis_size("tok"), axis=2)), "tok", 0, 0),
+        axis=1,
+    )
     mamba_out = summed_on_arrival(
         jnp.einsum("sdf,fo->dso", regrouped, out_weight, preferred_element_type=jnp.float32).astype(
             jnp.bfloat16

time: 99.1 us -> 97.5 us (0.984)
  the two profiles are of different devices: /device:TPU:450 before, /device:TPU:194 now
where the time goes in v1:
time: 97.5 us; the launch traced here: 96.5 us
  starting transfers between devices  33.9 us (35%)
  waiting for transfers between devices  19 us (19%)
  local copies, waits for them, and re-layouts  13.3 us (14%)
  blocking collectives  12.6 us (13%)
  other arithmetic  9.34 us (10%)
  matrix products  7.29 us (7%)
  between operations  1.04 us (1%)
    all_to_all x2, waiting for transfers between devices, summed_on_arrival(): lax.all_to_all(parts, axis, split_axis=0, concat_axis=0, tiled=True)  15.2 us
    all_to_all x2, starting transfers between devices, summed_on_arrival(): lax.all_to_all(parts, axis, split_axis=0, concat_axis=0, tiled=True)  15.1 us
    all_gather x1, blocking collectives, sent_together(): filled = lax.all_gather(both, axis, axis=dim, tiled=True)  12.6 us
    all_to_all x2, starting transfers between devices, in_one_piece(): lax.all_to_all(both, axis, split_axis=split_dim, concat_axis=concat_dim,...  9.59 us
    reshape x2, local copies, waits for them, and re-layouts, in_blocks(): return jnp.moveaxis(array.reshape(*before, count, -1, *after), dim, 0)  4.9 us
    all_to_all x1, starting transfers between devices, body(): lax.all_to_all(jnp.stack(jnp.split(normed, lax.axis_size('tok'), axis=2))...  4.71 us
    all_to_all x1, starting transfers between devices, from_everyone(): return lax.all_to_all(copies, axis, split_axis=0, concat_axis=0, tiled=True)  4.5 us
    all_to_all x1, waiting for transfers between devices, body(): lax.all_to_all(jnp.stack(jnp.split(normed, lax.axis_size('tok'), axis=2))...  3.11 us
  transfers between devices with their start and end apart: 6, of which 4 were waited for; matrix products, arithmetic and copies ran while one was open for 26% of the time, Pallas kernels for 0%

profile of v1, /device:TPU:194, one launch (start us, length us, event | category | flops | bytes accessed | tf_op | source)
XLA Modules:
  0.0 96.5 jit_solution(2423926541989380240)
XLA Ops:
  0.7 0.9 pad_maximum_fusion.3
  1.7 0.8 reshape.241
  2.4 4.8 %all-to-all-start = ((bf16[4,2,1024]{2,1,0:T(2,128)(2,1)}), bf16[4,2,1024]{2,1,0:T(2,128)(2,1)S(1)}, u32[]{:S(2)}, u32[]{:S(2)}) async-start(bf16[4,2,1024]{2,1,0:T(2,128)(2,1)} %reshape.241), calls=%async_computation | async-start | bytes 32768 | tf_op jit(solution)/shard_map/all_to_all | solution.py:13
  7.4 0.9 pad_maximum_fusion.1
  8.3 12.6 %all_gather.3 = bf16[2,64,1040]{2,1,0:T(8,128)(2,1)S(1)} all-gather(bf16[2,16,1040]{2,1,0:T(8,128)(2,1)S(1)} %pad_maximum_fusion.1), channel_id=1, replica_groups=mesh['dp'=16,'head'=8,'tok'=4] {'tok'}, dimensions={1}, use_global_device_ids=true | all-gather | bytes 332800 | tf_op jit(solution)/shard_map/all_gather | solution.py:20
  20.9 0.7 iota_compare_fusion.1
  21.6 0.7 broadcast_compare_fusion.1
  22.4 0.8 select_reduce_fusion
  24.1 0.7 broadcast_in_dim.109
  24.8 4.5 %all-to-all-start.4 = ((bf16[4,2,16,512]{3,2,1,0:T(8,128)(2,1)}), bf16[4,2,16,512]{3,2,1,0:T(8,128)(2,1)S(1)}, u32[]{:S(2)}, u32[]{:S(2)}) async-start(bf16[4,2,16,512]{3,2,1,0:T(8,128)(2,1)} %broadcast_in_dim.109), calls=%async_computation.4 | async-start | bytes 262144 | tf_op jit(solution)/shard_map/all_to_all | solution.py:37
  30.2 1.3 %fusion.6 = bf16[2,64,16,64]{1,3,2,0:T(8,128)(2,1)S(1)} fusion(f32[2,64,16,64]{1,3,2,0:T(8,128)S(1)} %convolution_bitcast_fusion, bf16[2,64,32,1]{2,1,3,0:T(8,128)(2,1)S(1)} %bitcast.69, bf16[2,16,64,32]{2,3,1,0:T(8,128)(2,1)} %param.25, f32[2,64,16]{1,2,0:T(8,128)S(1)} %copy.77), kind=kOutput, calls=%fused_computation.11 | convolution fusion | flops 8781824 | bytes 933888 | tf_op jit(solution)/shard_map/bsn,bhpn->bshp/dot_general | solution.py:115
  32.3 0.7 copy.80
  33.0 0.7 all-to-all-done.4
  33.8 4.8 %all-to-all-start.1 = ((bf16[4,2,16,1024]{3,2,1,0:T(8,128)(2,1)}), bf16[4,2,16,1024]{3,2,1,0:T(8,128)(2,1)S(1)}, u32[]{:S(2)}, u32[]{:S(2)}) async-start(bf16[4,2,16,1024]{3,2,1,0:T(8,128)(2,1)} %copy.80), calls=%async_computation.1 | async-start | bytes 524288 | tf_op jit(solution)/shard_map/all_to_all | solution.py:31
  38.7 1.6 %fusion.2 = (f32[2,256]{1,0:T(2,128)S(1)}, f32[2,256,1024]{2,1,0:T(8,128)S(1)}) fusion(pred[2,1024]{1,0:T(4,128)(4,1)S(1)} %broadcast_compare_fusion.1, bf16[2,256,128]{2,1,0:T(8,128)(2,1)S(1)} %reshape_reshape.3, bf16[2,1024,128]{2,1,0:T(8,128)(2,1)} %param.30), kind=kOutput, calls=%fused_computation.5 | convolution fusion | flops 135790080 | bytes 2756608 | tf_op jit(solution)/shard_map/cmq,czq->cmz/dot_general | solution.py:149
  40.8 0.6 fusion.4
  41.5 0.7 fusion.8
  42.8 1.1 %all-to-all-done.1 = bf16[4,2,16,1024]{3,2,1,0:T(8,128)(2,1)S(1)} async-done(((bf16[4,2,16,1024]{3,2,1,0:T(8,128)(2,1)}), bf16[4,2,16,1024]{3,2,1,0:T(8,128)(2,1)S(1)}, u32[]{:S(2)}, u32[]{:S(2)}) %all-to-all-start.1) | async-done | bytes 262176 | tf_op jit(solution)/shard_map/all_to_all | solution.py:31
  44.8 4.7 %all-to-all-start.2 = ((bf16[4,2,16,256]{3,2,1,0:T(8,128)(2,1)}), bf16[4,2,16,256]{3,2,1,0:T(8,128)(2,1)S(1)}, u32[]{:S(2)}, u32[]{:S(2)}) async-start(bf16[4,2,16,256]{3,2,1,0:T(8,128)(2,1)} %pad_maximum_fusion.2), calls=%async_computation.2 | async-start | bytes 131072 | tf_op jit(solution)/shard_map/all_to_all | solution.py:131
  49.5 1.1 %pad_maximum_fusion = bf16[1,2,64,520]{3,1,0,2:T(2,128)(2,1)} fusion(bf16[1,2,64,512]{3,1,0,2:T(2,128)(2,1)S(1)} %copy.87, bf16[1,2,64,4]{3,1,0,2:T(2,128)(2,1)S(1)} %copy.86, bf16[1,2,64,4]{3,1,0,2:T(2,128)(2,1)S(1)} %copy.85), kind=kLoop, calls=%fused_computation.41 | loop fusion | flops 399360 | bytes 266240 | tf_op jit(solution)/shard_map/concatenate | solution.py:12
  50.6 3.1 %all-to-all-done.2 = bf16[4,2,16,256]{3,2,1,0:T(8,128)(2,1)S(1)} async-done(((bf16[4,2,16,256]{3,2,1,0:T(8,128)(2,1)}), bf16[4,2,16,256]{3,2,1,0:T(8,128)(2,1)S(1)}, u32[]{:S(2)}, u32[]{:S(2)}) %all-to-all-start.2) | async-done | bytes 65568 | tf_op jit(solution)/shard_map/all_to_all | solution.py:131
  53.7 4.8 %all-to-all-start.5 = ((bf16[1,2,64,520]{3,1,0,2:T(2,128)(2,1)}), bf16[1,2,64,520]{3,1,0,2:T(2,128)(2,1)S(1)}, u32[]{:S(2)}, u32[]{:S(2)}) async-start(bf16[1,2,64,520]{3,1,0,2:T(2,128)(2,1)} %pad_maximum_fusion), calls=%async_computation.5 | async-start | bytes 327680 | tf_op jit(solution)/shard_map/all_to_all | solution.py:13
  58.9 1.5 %reshape.238 = bf16[32,2,2,4096]{3,1,0,2:T(2,128)(2,1)} reshape(bf16[64,2,4096]{2,0,1:T(8,128)(2,1)S(1)} %fusion) | data formatting | bytes 2097152 | tf_op jit(solution)/shard_map/reshape | solution.py:26
  60.4 3.4 %copy.82 = bf16[32,2,2,4096]{3,1,2,0:T(2,128)(2,1)} copy(bf16[32,2,2,4096]{3,1,0,2:T(2,128)(2,1)} %reshape.238) | data formatting | bytes 2097152 | tf_op jit(solution)/shard_map/reshape | solution.py:26
  63.8 10.2 %all-to-all-start.3 = ((bf16[32,2,2,4096]{3,1,2,0:T(2,128)(2,1)}), bf16[32,2,2,4096]{3,1,2,0:T(2,128)(2,1)S(1)}, u32[]{:S(2)}, u32[]{:S(2)}) async-start(bf16[32,2,2,4096]{3,1,2,0:T(2,128)(2,1)} %copy.82), calls=%async_computation.3 | async-start | bytes 2097152 | tf_op jit(solution)/shard_map/all_to_all | solution.py:31
  74.2 2.2 %fusion.7 = bf16[2,16,64,32]{2,3,1,0:T(8,128)(2,1)} fusion(bf16[2,64,16,64]{1,3,2,0:T(8,128)(2,1)} %bitcast.64, bf16[2,16,64,32]{2,3,1,0:T(8,128)(2,1)} %param.25, f32[2,64,16]{1,2,0:T(8,128)S(1)} %copy.89, f32[2,64,32]{1,2,0:T(8,128)S(1)} %copy.88, f32[2,16]{1,0:T(2,128)S(1)} %exp.39), kind=kOutput, calls=%fused_computation.13 | convolution fusion | flops 8716288 | bytes 548992 | tf_op jit(solution)/shard_map/brh,brhp,brn->bhpn/dot_general | solution.py:69
  76.6 0.9 mul.139
  77.6 1.1 %mul.140 = f32[4,2,16,512]{3,1,2,0:T(2,128)S(1)} reshape(f32[4,2,16,4,128]{4,3,1,2,0:T(4,128)} %mul.139) | data formatting | bytes 524288 | tf_op jit(solution)/shard_map/mul | solution.py:202
  78.9 1.2 %multiply_reduce_fusion = f32[2,16,512]{2,0,1:T(2,128)S(1)} fusion(f32[4,2,16,512]{3,1,2,0:T(2,128)S(1)} %mul.140, bf16[4,2,16,520]{3,1,2,0:T(2,128)(2,1)} %bitcast.62), kind=kLoop, calls=%fused_computation.38 | loop fusion | flops 180224 | bytes 458752 | tf_op jit(solution)/shard_map/reduce_sum | solution.py:202
  80.8 14.1 %all-to-all-done.3 = bf16[32,2,2,4096]{3,1,2,0:T(2,128)(2,1)S(1)} async-done(((bf16[32,2,2,4096]{3,1,2,0:T(2,128)(2,1)}), bf16[32,2,2,4096]{3,1,2,0:T(2,128)(2,1)S(1)}, u32[]{:S(2)}, u32[]{:S(2)}) %all-to-all-start.3) | async-done | bytes 1048608 | tf_op jit(solution)/shard_map/all_to_all | solution.py:31
  94.9 1.0 %reduce_sum.77 = bf16[2,2,4096]{2,0,1:T(2,128)(2,1)S(1)} reduce(bf16[32,2,2,4096]{3,1,2,0:T(2,128)(2,1)S(1)} %all-to-all-done.3, bf16[]{:T(256)} %constant.10.clone.1), dimensions={0}, to_apply=%region_3.4 | reduce | flops 507904 | bytes 1081346 | tf_op jit(solution)/shard_map/reduce_sum | solution.py:32
  95.9 0.7 copy.91
  (80 shorter events, 6.5 us)
Async XLA Ops:
  0.6 57.8 %copy-start = (bf16[256,4096]{1,0:T(8,128)(2,1)S(1)}, bf16[256,4096]{1,0:T(8,128)(2,1)}, u32[]{:S(2)}) copy-start(bf16[256,4096]{1,0:T(8,128)(2,1)} %param.26) | copy-start | bytes 6291460
  0.6 23.3 %copy-start.9 = (f32[16]{0:T(128)S(1)}, f32[16]{0:T(128)}, u32[]{:S(2)}) copy-start(f32[16]{0:T(128)} %param.23) | copy-start | bytes 196
  0.7 23.4 %copy-start.5 = (bf16[2,16,512]{2,1,0:T(8,128)(2,1)S(1)}, bf16[2,16,512]{2,1,0:T(8,128)(2,1)}, u32[]{:S(2)}) copy-start(bf16[2,16,512]{2,1,0:T(8,128)(2,1)} %param.27) | copy-start | bytes 98308
  2.4 21.6 %all-to-all-start = ((bf16[4,2,1024]{2,1,0:T(2,128)(2,1)}), bf16[4,2,1024]{2,1,0:T(2,128)(2,1)S(1)}, u32[]{:S(2)}, u32[]{:S(2)}) async-start(bf16[4,2,1024]{2,1,0:T(2,128)(2,1)} %reshape.241), calls=%async_computation | async-start | bytes 32768 | tf_op jit(solution)/shard_map/all_to_all | solution.py:13
  23.8 6.4 %copy-start.2 = (bf16[2,64,1024]{1,2,0:T(8,128)(2,1)}, bf16[2,64,1024]{1,2,0:T(8,128)(2,1)S(1)}, u32[]{:S(2)}) copy-start(bf16[2,64,1024]{1,2,0:T(8,128)(2,1)S(1)} %copy.68) | copy-start | bytes 786436
  24.8 9.0 %all-to-all-start.4 = ((bf16[4,2,16,512]{3,2,1,0:T(8,128)(2,1)}), bf16[4,2,16,512]{3,2,1,0:T(8,128)(2,1)S(1)}, u32[]{:S(2)}, u32[]{:S(2)}) async-start(bf16[4,2,16,512]{3,2,1,0:T(8,128)(2,1)} %broadcast_in_dim.109), calls=%async_computation.4 | async-start | bytes 262144 | tf_op jit(solution)/shard_map/all_to_all | solution.py:37
  32.3 8.1 %copy-start.6 = (bf16[2,16,128]{2,1,0:T(8,128)(2,1)S(1)}, bf16[2,16,128]{2,1,0:T(8,128)(2,1)}, u32[]{:S(2)}) copy-start(bf16[2,16,128]{2,1,0:T(8,128)(2,1)} %param.28) | copy-start | bytes 24580
  33.0 7.5 %copy-start.7 = (bf16[2,16,128]{2,1,0:T(8,128)(2,1)S(1)}, bf16[2,16,128]{2,1,0:T(8,128)(2,1)}, u32[]{:S(2)}) copy-start(bf16[2,16,128]{2,1,0:T(8,128)(2,1)} %param.29) | copy-start | bytes 24580
  33.8 10.1 %all-to-all-start.1 = ((bf16[4,2,16,1024]{3,2,1,0:T(8,128)(2,1)}), bf16[4,2,16,1024]{3,2,1,0:T(8,128)(2,1)S(1)}, u32[]{:S(2)}, u32[]{:S(2)}) async-start(bf16[4,2,16,1024]{3,2,1,0:T(8,128)(2,1)} %copy.80), calls=%async_computation.1 | async-start | bytes 524288 | tf_op jit(solution)/shard_map/all_to_all | solution.py:31
  38.7 2.8 %copy-start.10 = (bf16[2,1024,128]{2,1,0:T(8,128)(2,1)S(1)}, bf16[2,1024,128]{2,1,0:T(8,128)(2,1)}, u32[]{:S(2)}) copy-start(bf16[2,1024,128]{2,1,0:T(8,128)(2,1)} %param.31) | copy-start | bytes 1572868
  41.5 2.4 %copy-start.3 = (bf16[2,16,1024]{2,1,0:T(8,128)(2,1)S(1)}, bf16[2,16,1024]{2,1,0:T(8,128)(2,1)}, u32[]{:S(2)}) copy-start(bf16[2,16,1024]{2,1,0:T(8,128)(2,1)} %param.17) | copy-start | bytes 196612
  41.5 2.4 %copy-start.4 = (bf16[2,16,1024]{2,1,0:T(8,128)(2,1)S(1)}, bf16[2,16,1024]{2,1,0:T(8,128)(2,1)}, u32[]{:S(2)}) copy-start(bf16[2,16,1024]{2,1,0:T(8,128)(2,1)} %param.18) | copy-start | bytes 196612
  41.5 2.5 %copy-start.8 = (f32[1024]{0:T(1024)S(1)}, f32[1024]{0:T(1024)}, u32[]{:S(2)}) copy-start(f32[1024]{0:T(1024)} %param.24) | copy-start | bytes 12292
  44.8 8.9 %all-to-all-start.2 = ((bf16[4,2,16,256]{3,2,1,0:T(8,128)(2,1)}), bf16[4,2,16,256]{3,2,1,0:T(8,128)(2,1)S(1)}, u32[]{:S(2)}, u32[]{:S(2)}) async-start(bf16[4,2,16,256]{3,2,1,0:T(8,128)(2,1)} %pad_maximum_fusion.2), calls=%async_computation.2 | async-start | bytes 131072 | tf_op jit(solution)/shard_map/all_to_all | solution.py:131
  53.7 10.1 %all-to-all-start.5 = ((bf16[1,2,64,520]{3,1,0,2:T(2,128)(2,1)}), bf16[1,2,64,520]{3,1,0,2:T(2,128)(2,1)S(1)}, u32[]{:S(2)}, u32[]{:S(2)}) async-start(bf16[1,2,64,520]{3,1,0,2:T(2,128)(2,1)} %pad_maximum_fusion), calls=%async_computation.5 | async-start | bytes 327680 | tf_op jit(solution)/shard_map/all_to_all | solution.py:13
  63.8 12.8 %copy-start.1 = (bf16[1,2,64,520]{3,1,0,2:T(2,128)(2,1)}, bf16[1,2,64,520]{3,1,0,2:T(2,128)(2,1)S(1)}, u32[]{:S(2)}) copy-start(bf16[1,2,64,520]{3,1,0,2:T(2,128)(2,1)S(1)} %all-to-all-done.5) | copy-start | bytes 399364
  63.8 31.1 %all-to-all-start.3 = ((bf16[32,2,2,4096]{3,1,2,0:T(2,128)(2,1)}), bf16[32,2,2,4096]{3,1,2,0:T(2,128)(2,1)S(1)}, u32[]{:S(2)}, u32[]{:S(2)}) async-start(bf16[32,2,2,4096]{3,1,2,0:T(2,128)(2,1)} %copy.82), calls=%async_computation.3 | async-start | bytes 2097152 | tf_op jit(solution)/shard_map/all_to_all | solution.py:31
